TPU v7x, 1024 devices: a whole 4x4x32 slice. The times are simulated.
1024 devices in a mesh: seq: 16 (over x, y), grp: 64 (over z, core).
Axes of the slice: x: 4, y: 4, z: 32, core: 2. Of those that a mesh axis runs over, the one named last changes fastest.
Arguments:
- p_x: bfloat16 [64, 4096, 2048], P('grp', 'seq'), may hold values from -6 to 6
- p_bc: bfloat16 [64, 4096, 256], P('grp', 'seq'), may hold values from -4 to 4
- p_dt: float32 [64, 32, 4096], P('grp', None, 'seq'), may hold values from 0.005 to 0.04
- p_decay: float32 [64, 32, 4096], P('grp', None, 'seq'), may hold values from -1 to 0
- r_x: bfloat16 [131072, 2048], P('grp', 'seq'), may hold values from -6 to 6
- r_bc: bfloat16 [131072, 256], P('grp'), may hold values from -4 to 4
- r_dt: float32 [32, 131072], P('seq', 'grp'), may hold values from 0.005 to 0.04
- r_decay: float32 [32, 131072], P('seq', 'grp'), may hold values from -1 to 0
- pack_list: int32 [64, 8], P('grp'), may hold values from -1 to 383, as said below
- resp_len: int32 [384], replicated, may hold values from 32 to 256, as said below
- resp_prompt: int32 [384], replicated, may hold values from 0 to 63, as said below
- d_skip: float32 [32], replicated, may hold values from 0.5 to 1.5
Outputs:
- p_out: bfloat16 [64, 4096, 2048], P('grp', 'seq')
- r_out: bfloat16 [131072, 2048], P('grp', 'seq')
Inputs may be any that keep to these rules, and one draw needn't show every extreme that they name: `pack_list`: row g lists the responses placed on index g of grp in the order of their rows, -1 marking an empty slot; every response stands in exactly one slot. `resp_len`: a device's responses take its rows one after another from its first row in slot order; the rows after them are unused. `resp_prompt`: every prompt has exactly 6 responses.
All inputs are finite; a program needn't handle non-finite values.
Results may differ from a plain program's by a relative error of at most 0.0053.
Values may be sent and summed in bfloat16 or wider, within the bound.
No kernel may reach another device: no remote copies, remote signals or barrier semaphores. Data moves between devices by JAX's collectives and lax.ppermute only.
A program may use at most 64 MiB of HBM per device.

v0:
```python
import jax
import jax.numpy as jnp
from jax import lax
from jax.sharding import PartitionSpec as P

STRETCH = 256


def carried_in(value, axis, join, neutral):
    count, mine = (lax.axis_size(axis), lax.axis_index(axis))
    pieces = jax.tree.map(lambda part: lax.all_gather(part, axis), value)
    total = jax.tree.map(
        lambda part, zero: jnp.full_like(part, 0) + jnp.asarray(zero, part.dtype), value, neutral
    )

    def turn(position, total):
        longer = join(total, jax.tree.map(lambda part: part[position], pieces))
        return jax.tree.map(lambda new, old: jnp.where(position < mine, new, old), longer, total)

    return lax.fori_loop(0, count - 1, turn, total)


def from_root(value, axis, source):
    kept = jnp.where(lax.axis_index(axis) == source, value, 0).astype(value.dtype)
    return lax.psum(kept, axis)


def product(einsum_form, left_side, right_side):
    return jnp.einsum(einsum_form, left_side, right_side, preferred_element_type=jnp.float32)


def block_terms(block_x, block_bc, block_dt, block_decay, block_slot):
    length = block_x.shape[0]
    head_count = block_dt.shape[0]
    state_width = block_bc.shape[1] // 2
    inputs = block_x.reshape(length, head_count, -1)
    b_rows = block_bc[:, :state_width]
    c_rows = block_bc[:, state_width:]
    running = jnp.cumsum(block_decay, axis=1)
    before = running - block_decay
    places = jnp.arange(length)
    same_span = (block_slot[:, None] == block_slot[None, :]) & (places[None, :] <= places[:, None])
    starts_here = jnp.concatenate([jnp.ones((1,), jnp.bool_), block_slot[1:] != block_slot[:-1]])
    leader = same_span & starts_here[None, :]
    offset = jnp.sum(jnp.where(leader[None], before[:, None, :], 0.0), axis=2)
    gained = running - offset
    scores = jnp.dot(c_rows, b_rows.T, preferred_element_type=jnp.float32)
    spread = jnp.where(same_span[None], running[:, :, None] - running[:, None, :], -jnp.inf)
    mixing = (jnp.exp(spread) * block_dt[:, None, :] * scores[None]).astype(jnp.bfloat16)
    inner_part = product("hij,jhp->ihp", mixing, inputs)
    tail_rows = block_slot == block_slot[length - 1]
    to_end = jnp.where(tail_rows[None], jnp.exp(running[:, length - 1 :] - running) * block_dt, 0.0)
    scaled = (to_end[:, :, None] * b_rows[None].astype(jnp.float32)).astype(jnp.bfloat16)
    local_state = product("hjn,jhp->hnp", scaled, inputs)
    return (inputs, inner_part, gained, local_state, c_rows)


def response_layer(skip_gain, rows_x, rows_bc, rows_dt, rows_decay, row_slot, slot_seeds):
    slot_count = slot_seeds.shape[0]
    blocks = rows_x.shape[0] // STRETCH
    head_count = rows_dt.shape[0]
    sliced = (
        rows_x.reshape(blocks, STRETCH, -1),
        rows_bc.reshape(blocks, STRETCH, -1),
        rows_dt.reshape(head_count, blocks, STRETCH).transpose(1, 0, 2),
        rows_decay.reshape(head_count, blocks, STRETCH).transpose(1, 0, 2),
        row_slot.reshape(blocks, STRETCH),
    )
    slot_ids = jnp.arange(slot_count)

    def advance(carry_pair, pieces):
        carried_state, previous = carry_pair
        block_slot = pieces[4]
        inputs, inner_part, gained, local_state, c_rows = block_terms(
            pieces[0], pieces[1], pieces[2], pieces[3], block_slot
        )
        first_slot = block_slot[0]
        carried_on = first_slot == previous
        chosen = (slot_ids == first_slot) & carried_on
        bases_table = jnp.where(
            chosen[:, None, None, None], carried_state.astype(jnp.bfloat16)[None], slot_seeds
        )
        projected = product("in,khnp->ikhp", c_rows, bases_table)
        hot_rows = (block_slot[:, None] == slot_ids[None, :]).astype(jnp.float32)
        carried = (
            jnp.sum(projected * hot_rows[:, :, None, None], axis=1) * jnp.exp(gained).T[:, :, None]
        )
        output = inner_part + carried + skip_gain[None, :, None] * inputs.astype(jnp.float32)
        output = jnp.where((block_slot < slot_count)[:, None, None], output, 0.0)
        final_slot = block_slot[STRETCH - 1]
        fresh_seed = jnp.sum(
            jnp.where(
                (slot_ids == final_slot)[:, None, None, None], slot_seeds.astype(jnp.float32), 0.0
            ),
            axis=0,
        )
        anchor = jnp.where((final_slot == first_slot) & carried_on, carried_state, fresh_seed)
        carried_state = jnp.exp(gained[:, -1])[:, None, None] * anchor + local_state
        return ((carried_state, final_slot), output.reshape(STRETCH, -1).astype(jnp.bfloat16))

    initial = (jnp.zeros(slot_seeds.shape[1:], jnp.float32), jnp.int32(-1))
    final_pair, outputs = lax.scan(advance, initial, sliced)
    return outputs.reshape(rows_x.shape)


def slot_layout(pack_row, resp_len, resp_prompt, row_count):
    hit_table = pack_row[:, None] == jnp.arange(resp_len.shape[0])[None, :]
    slot_spans = jnp.sum(jnp.where(hit_table, resp_len[None, :], 0), axis=1)
    owners = jnp.where(
        pack_row >= 0, jnp.sum(jnp.where(hit_table, resp_prompt[None, :], 0), axis=1), -1
    )
    limits = jnp.cumsum(slot_spans)
    row_slot = jnp.sum(
        (jnp.arange(row_count)[:, None] >= limits[None, :]).astype(jnp.int32), axis=1
    )
    return (row_slot, owners)


def combine(earlier, later_part):
    return (earlier[0] * later_part[0], later_part[0][:, None, None] * earlier[1] + later_part[1])


def on_device(
    p_x, p_bc, p_dt, p_decay, r_x, r_bc, r_dt, r_decay, pack_list, resp_len, resp_prompt, d_skip
):
    head_count = p_dt.shape[1]
    groups = lax.axis_size("seq")
    block_heads = head_count // groups
    state_width = p_bc.shape[2] // 2
    channels = p_x.shape[2] // head_count
    pieces_list = block_terms(
        p_x[0, 0:STRETCH],
        p_bc[0, 0:STRETCH],
        p_dt[0, :, 0:STRETCH],
        p_decay[0, :, 0:STRETCH],
        jnp.zeros((STRETCH,), jnp.int32),
    )
    local_end = jnp.zeros((head_count, state_width, channels), jnp.float32)
    local_end = jnp.exp(pieces_list[2][:, -1])[:, None, None] * local_end + pieces_list[3]
    decay_total = jnp.exp(jnp.sum(p_decay[0], axis=1))
    ahead_pair = carried_in(
        (decay_total, local_end),
        "seq",
        combine,
        (jnp.ones_like(decay_total), jnp.zeros_like(local_end)),
    )
    prefix = ahead_pair[1]
    whole_state = combine(ahead_pair, (decay_total, local_end))[1]
    final_state = from_root(whole_state.astype(jnp.bfloat16), "seq", groups - 1)
    own_seed = lax.dynamic_slice_in_dim(
        final_state, lax.axis_index("seq") * block_heads, block_heads, 0
    )
    inputs, inner_part, gained, local_state, c_rows = pieces_list
    carried = (
        product("in,hnp->ihp", c_rows, prefix.astype(jnp.bfloat16)) * jnp.exp(gained).T[:, :, None]
    )
    output = inner_part + carried + d_skip[None, :, None] * inputs.astype(jnp.float32)
    outputs = output.reshape(STRETCH, -1).astype(jnp.bfloat16)
    p_out = outputs[None]
    row_slot, owners = slot_layout(pack_list[0], resp_len, resp_prompt, r_x.shape[0])
    gathered_piece = lax.all_gather(own_seed[None], "grp", axis=0, tiled=True)
    chosen = (owners[:, None] == jnp.arange(gathered_piece.shape[0])[None, :]).astype(jnp.bfloat16)
    slot_seeds = product("km,mhnp->khnp", chosen, gathered_piece).astype(jnp.bfloat16)
    skip_block = lax.dynamic_slice_in_dim(
        d_skip, lax.axis_index("seq") * block_heads, block_heads, 0
    )
    r_out = response_layer(skip_block, r_x, r_bc, r_dt, r_decay, row_slot, slot_seeds)
    return (p_out, r_out)


def solution(mesh):
    placed = (
        P("grp", "seq", None),
        P("grp", "seq", None),
        P("grp", None, "seq"),
        P("grp", None, "seq"),
        P("grp", "seq"),
        P("grp", None),
        P("seq", "grp"),
        P("seq", "grp"),
        P("grp", None),
        P(),
        P(),
        P(),
    )
    return jax.shard_map(
        on_device,
        mesh=mesh,
        in_specs=placed,
        out_specs=(P("grp", "seq", None), P("grp", "seq")),
        check_vma=False,
    )
```

profile of v0, /device:TPU:1, one launch (start us, length us, event | category | flops | bytes accessed | tf_op | source)
XLA Modules:
  0.0 665.0 jit_solution(15510527633113798931)
XLA Ops:
  13.7 1.5 copy.80
  15.2 2.5 fusion.44
  19.9 34.2 %all-reduce = f32[512]{0:T(512)S(1)} all-reduce(f32[512]{0:T(512)S(1)} %get-tuple-element.409), channel_id=2, replica_groups=mesh['seq'=16,'grp'=64] {'seq'}, use_global_device_ids=true, to_apply=%add | all-reduce | flops 512 | bytes 4096
  54.2 118.8 %all-gather.6.cloned.1.call-done = f32[512,128,64]{1,2,0:T(8,128)} async-done(((f32[32,128,64]{1,2,0:T(8,128)}), f32[512,128,64]{1,2,0:T(8,128)}) %all-gather.6.cloned.1.call-update) | async-done | bytes 16777232 | tf_op jit(solution)/shard_map/all_gather | solution.py:11
  173.1 76.6 %while.30 = (s32[]{:T(128)}, f32[32,128,64]{2,1,0:T(8,128)}, s32[]{:T(128)}, f32[16,32]{1,0:T(8,128)S(1)}, f32[16,32,128,64]{2,3,1,0:T(8,128)}, /*index=5*/s32[]{:T(128)}, s32[]{:T(128)}) while((s32[]{:T(128)}, f32[32,128,64]{2,1,0:T(8,128)}, s32[]{:T(128)}, f32[16,32]{1,0:T(8,128)S(1)}, f32[16,32,128,64]{2,3,1,0:T(8,128)}, ...), condition=%wide.region_5.6_spmd.clone, body=%wide.region_4.5_spmd.clone.sunk | while | flops 1048580 | bytes 7340521 | solution.py:20
  173.1 1.3 constant_dynamic-slice_fusion.12
  175.0 1.7 fusion.83
  176.7 1.3 constant_dynamic-slice_fusion.12
  178.6 3.3 fusion.83
  183.8 3.3 fusion.83
  189.1 3.3 fusion.83
  194.3 3.3 fusion.83
  199.5 3.3 fusion.83
  204.7 3.3 fusion.83
  209.9 3.3 fusion.83
  215.1 3.3 fusion.83
  220.3 3.3 fusion.83
  223.6 1.3 constant_dynamic-slice_fusion.12
  225.5 3.3 fusion.83
  230.8 3.3 fusion.83
  236.0 3.3 fusion.83
  241.2 3.3 fusion.83
  246.4 3.3 fusion.83
  249.7 2.2 copy.83
  251.9 2.4 fusion.50
  254.4 155.9 %all-reduce.3.cloned.1.call-done = bf16[32,128,64]{1,2,0:T(8,128)(2,1)} async-done(((bf16[32,128,64]{1,2,0:T(8,128)(2,1)}), bf16[32,128,64]{1,2,0:T(8,128)(2,1)}) %all-reduce.3.cloned.1.call-update) | async-done | bytes 524304 | tf_op jit(solution)/shard_map/psum | solution.py:25
  410.3 1.4 constant_dynamic-slice_fusion.6
  413.8 3.1 fusion.39
  416.9 1.4 copy.88
  418.3 133.6 %all-gather.8.cloned.1.call-done = bf16[128,128,64]{1,2,0:T(8,128)(2,1)} async-done(((bf16[2,128,64]{1,2,0:T(8,128)(2,1)}), bf16[128,128,64]{1,2,0:T(8,128)(2,1)}) %all-gather.8.cloned.1.call-update) | async-done | bytes 2097168 | tf_op jit(solution)/shard_map/all_gather | solution.py:161
  551.9 2.8 fusion.45
  554.7 103.7 %while.31 = (s32[]{:T(128)}, f32[2,128,64]{1,2,0:T(8,128)S(1)}, s32[]{:T(128)}, bf16[8,256,128]{2,1,0:T(8,128)(2,1)}, f32[8,2,256]{2,1,0:T(2,128)}, /*index=5*/s...) while((s32[]{:T(128)}, f32[2,128,64]{1,2,0:T(8,128)S(1)}, ...), condition=%wide.region_17.18_spmd.clone.clone, body=%wide.region_11.17_spmd.clone.clone.sunk | while | flops 111778848 | bytes 3553738 | solution.py:102
  (364 shorter events, 117.8 us)
Async XLA Ops:
  7.2 165.9 %all-gather.6.cloned.1.call-start = ((), (), s32[]{:S(2)}) async-start(), calls=%async_computation.1 | async-start | bytes 17825792 | tf_op jit(solution)/shard_map/all_gather | solution.py:11
  15.2 157.9 %copy-start.1 = (bf16[1,256,2048]{1,2,0:T(8,128)(2,1)}, bf16[1,256,2048]{1,2,0:T(8,128)(2,1)S(1)}, u32[]{:S(2)}) copy-start(bf16[1,256,2048]{1,2,0:T(8,128)(2,1)S(1)} %copy.80) | copy-start | bytes 3145732
  15.2 2.6 copy-start.4
  17.7 392.6 %all-reduce.3.cloned.1.call-start = ((), (), s32[]{:S(2)}) async-start(), calls=%async_computation | async-start | bytes 1048576 | tf_op jit(solution)/shard_map/psum | solution.py:25
  251.8 159.9 %copy-start.9 = (f32[32]{0:T(128)S(1)}, f32[32]{0:T(128)}, u32[]{:S(2)}) copy-start(f32[32]{0:T(128)} %param.27) | copy-start | bytes 388
  251.9 159.9 %copy-start.6 = (s32[384]{0:T(512)S(1)}, s32[384]{0:T(512)}, u32[]{:S(2)}) copy-start(s32[384]{0:T(512)} %param.26) | copy-start | bytes 4612
  251.9 159.9 %copy-start.7 = (s32[384]{0:T(512)S(1)}, s32[384]{0:T(512)}, u32[]{:S(2)}) copy-start(s32[384]{0:T(512)} %param.25) | copy-start | bytes 4612
  251.9 159.9 %copy-start.8 = (s32[1,8]{1,0:T(1,128)S(1)}, s32[1,8]{1,0:T(1,128)}, u32[]{:S(2)}) copy-start(s32[1,8]{1,0:T(1,128)} %param.24) | copy-start | bytes 100
  251.9 160.4 %copy-start.3 = (bf16[1,256,256]{2,1,0:T(8,128)(2,1)S(1)}, bf16[1,256,256]{2,1,0:T(8,128)(2,1)}, u32[]{:S(2)}) copy-start(bf16[1,256,256]{2,1,0:T(8,128)(2,1)} %param.17) | copy-start | bytes 393220
  251.9 160.6 %copy-start = (f32[32,128,64]{2,1,0:T(8,128)S(1)}, f32[32,128,64]{2,1,0:T(8,128)}, u32[]{:S(2)}) copy-start(f32[32,128,64]{2,1,0:T(8,128)} %get-tuple-element.164) | copy-start | bytes 3145732
  254.3 297.5 %all-gather.8.cloned.1.call-start = ((), (), s32[]{:S(2)}) async-start(), calls=%async_computation.2 | async-start | bytes 2129920 | tf_op jit(solution)/shard_map/all_gather | solution.py:161
  412.5 1.2 copy-start.2
  412.5 1.2 copy-start.5
Sparse Core Ops, SparseCore 0:
  17.8 155.2 all-gather.5
  254.5 155.7 all-reduce.2
  413.0 138.8 all-gather.7
where the time goes:
time: 668 us; the launch traced here: 665 us
  waiting for transfers between devices  408 us (61%)
  other arithmetic  93.6 us (14%)
  local copies, waits for them, and re-layouts  74.4 us (11%)
  blocking collectives  34.2 us (5%)
  loops' own time  21.4 us (3%)
  matrix products  18.2 us (3%)
  between operations  14.7 us (2%)
    psum x1, waiting for transfers between devices, from_root(): return lax.psum(kept, axis)  156 us
    all_gather x1, waiting for transfers between devices, on_device(): gathered_piece = lax.all_gather(own_seed[None], 'grp', axis=0, tiled=True)  134 us
    all_gather x1, waiting for transfers between devices, carried_in(): pieces = jax.tree.map(lambda part: lax.all_gather(part, axis), value)  119 us
    select_n x15, other arithmetic, turn(): jnp.where(position < mine, new, old)  47.5 us
    unnamed x1, blocking collectives  34.2 us
    dynamic_slice x30, local copies, waits for them, and re-layouts, turn(): longer = join(total, jax.tree.map(lambda part: part[position], pieces))  28.5 us
    another operation x1, loops' own time, response_layer(): final_pair, outputs = lax.scan(advance, initial, sliced)  21 us
    dot_general x28, matrix products, product(): jnp.einsum(einsum_form, left_side, right_side, preferred_element_type=jnp...  16.6 us
  transfers between devices with their start and end apart: 3, of which 3 were waited for; matrix products, arithmetic and copies ran while one was open for 1% of the time, Pallas kernels for 0%

commit v1 on v0

v1 whole, which is shorter than its diff:
```python
import jax
import jax.numpy as jnp
from jax import lax
from jax.sharding import PartitionSpec as P

STRETCH = 256


def product(einsum_form, left_side, right_side):
    return jnp.einsum(einsum_form, left_side, right_side, preferred_element_type=jnp.float32)


def block_terms(block_x, block_bc, block_dt, block_decay, block_slot):
    length = block_x.shape[0]
    head_count = block_dt.shape[0]
    state_width = block_bc.shape[1] // 2
    inputs = block_x.reshape(length, head_count, -1)
    b_rows = block_bc[:, :state_width]
    c_rows = block_bc[:, state_width:]
    running = jnp.cumsum(block_decay, axis=1)
    before = running - block_decay
    places = jnp.arange(length)
    same_span = (block_slot[:, None] == block_slot[None, :]) & (places[None, :] <= places[:, None])
    starts_here = jnp.concatenate([jnp.ones((1,), jnp.bool_), block_slot[1:] != block_slot[:-1]])
    leader = same_span & starts_here[None, :]
    offset = jnp.sum(jnp.where(leader[None], before[:, None, :], 0.0), axis=2)
    gained = running - offset
    scores = jnp.dot(c_rows, b_rows.T, preferred_element_type=jnp.float32)
    spread = jnp.where(same_span[None], running[:, :, None] - running[:, None, :], -jnp.inf)
    mixing = (jnp.exp(spread) * block_dt[:, None, :] * scores[None]).astype(jnp.bfloat16)
    inner_part = product("hij,jhp->ihp", mixing, inputs)
    tail_rows = block_slot == block_slot[length - 1]
    to_end = jnp.where(tail_rows[None], jnp.exp(running[:, length - 1 :] - running) * block_dt, 0.0)
    scaled = (to_end[:, :, None] * b_rows[None].astype(jnp.float32)).astype(jnp.bfloat16)
    local_state = product("hjn,jhp->hnp", scaled, inputs)
    return (inputs, inner_part, gained, local_state, c_rows)


def slot_layout(pack_row, resp_len, resp_prompt, row_count):
    hit_table = pack_row[:, None] == jnp.arange(resp_len.shape[0])[None, :]
    slot_spans = jnp.sum(jnp.where(hit_table, resp_len[None, :], 0), axis=1)
    owners = jnp.where(
        pack_row >= 0, jnp.sum(jnp.where(hit_table, resp_prompt[None, :], 0), axis=1), -1
    )
    limits = jnp.cumsum(slot_spans)
    row_slot = jnp.sum(
        (jnp.arange(row_count)[:, None] >= limits[None, :]).astype(jnp.int32), axis=1
    )
    return (row_slot, owners)


def prompt_part(p_x, p_bc, p_dt, p_decay, d_skip):
    head_count = p_dt.shape[1]
    groups = lax.axis_size("seq")
    block_heads = head_count // groups
    state_width = p_bc.shape[2] // 2
    inputs, inner_part, gained, local_state, c_rows = block_terms(
        p_x[0], p_bc[0], p_dt[0], p_decay[0], jnp.zeros((STRETCH,), jnp.int32)
    )
    channels = inputs.shape[2]
    block_gain = jnp.exp(gained[:, -1])
    pad = 8
    gain_rows = jnp.broadcast_to(block_gain[:, None, None], (head_count, pad, channels))
    payload = jnp.concatenate([local_state, gain_rows], axis=1)
    payload = payload.reshape(groups, block_heads, state_width + pad, channels)
    arrived = lax.all_to_all(payload, "seq", 0, 0, tiled=True)
    pieces = arrived[:, :, :state_width, :]
    gains = arrived[:, :, state_width, 0]
    state = jnp.zeros((block_heads, state_width, channels), jnp.float32)
    prefixes = []
    for position in range(groups):
        prefixes.append(state.astype(jnp.bfloat16))
        state = gains[position][:, None, None] * state + pieces[position]
    own_seed = state.astype(jnp.bfloat16)
    sent_back = jnp.stack(prefixes, axis=0)
    prefix = lax.all_to_all(sent_back, "seq", 0, 0, tiled=True)
    prefix = prefix.reshape(head_count, state_width, channels)
    carried = product("in,hnp->ihp", c_rows, prefix) * jnp.exp(gained).T[:, :, None]
    output = inner_part + carried + d_skip[None, :, None] * inputs.astype(jnp.float32)
    p_out = output.reshape(STRETCH, -1).astype(jnp.bfloat16)[None]
    return p_out, own_seed


def response_part(skip_gain, rows_x, rows_bc, rows_dt, rows_decay, row_slot, slot_seeds):
    slot_count = slot_seeds.shape[0]
    blocks = rows_x.shape[0] // STRETCH
    head_count = rows_dt.shape[0]
    state_width = rows_bc.shape[1] // 2
    sliced = (
        rows_x.reshape(blocks, STRETCH, -1),
        rows_bc.reshape(blocks, STRETCH, -1),
        rows_dt.reshape(head_count, blocks, STRETCH).transpose(1, 0, 2),
        rows_decay.reshape(head_count, blocks, STRETCH).transpose(1, 0, 2),
        row_slot.reshape(blocks, STRETCH),
    )
    inputs, inner_part, gained, local_state, c_rows = jax.vmap(block_terms)(*sliced)
    block_slot = sliced[4]
    channels = inputs.shape[3]
    slot_ids = jnp.arange(slot_count)
    seeds_f32 = slot_seeds.astype(jnp.float32)
    block_gain = jnp.exp(gained[:, :, -1])

    state = jnp.zeros((head_count, state_width, channels), jnp.float32)
    previous = jnp.int32(-1)
    continued_bases = []
    continued_flags = []
    for block in range(blocks):
        first_slot = block_slot[block, 0]
        final_slot = block_slot[block, STRETCH - 1]
        carried_on = first_slot == previous
        continued_bases.append(state.astype(jnp.bfloat16))
        continued_flags.append(carried_on)
        fresh_seed = jnp.sum(
            jnp.where((slot_ids == final_slot)[:, None, None, None], seeds_f32, 0.0), axis=0
        )
        anchor = jnp.where((final_slot == first_slot) & carried_on, state, fresh_seed)
        state = block_gain[block][:, None, None] * anchor + local_state[block]
        previous = final_slot
    continued_bases = jnp.stack(continued_bases, axis=0)
    continued_flags = jnp.stack(continued_flags, axis=0)

    hot_rows = (block_slot[:, :, None] == slot_ids[None, None, :]).astype(jnp.bfloat16)
    masked_c = (c_rows[:, :, None, :] * hot_rows[:, :, :, None]).reshape(
        blocks * STRETCH, slot_count * state_width
    )
    seed_table = slot_seeds.transpose(0, 2, 1, 3).reshape(
        slot_count * state_width, head_count * channels
    )
    from_seeds = jnp.dot(masked_c, seed_table, preferred_element_type=jnp.float32)
    from_seeds = from_seeds.reshape(blocks, STRETCH, head_count, channels)
    from_state = product("bin,bhnp->bihp", c_rows, continued_bases)
    continues_row = continued_flags[:, None] & (block_slot == block_slot[:, :1])
    projected = jnp.where(continues_row[:, :, None, None], from_state, from_seeds)
    carried = projected * jnp.exp(gained).transpose(0, 2, 1)[:, :, :, None]
    output = inner_part + carried + skip_gain[None, None, :, None] * inputs.astype(jnp.float32)
    output = jnp.where((block_slot < slot_count)[:, :, None, None], output, 0.0)
    return output.reshape(rows_x.shape).astype(jnp.bfloat16)


def on_device(
    p_x, p_bc, p_dt, p_decay, r_x, r_bc, r_dt, r_decay, pack_list, resp_len, resp_prompt, d_skip
):
    head_count = p_dt.shape[1]
    groups = lax.axis_size("seq")
    block_heads = head_count // groups
    p_out, own_seed = prompt_part(p_x, p_bc, p_dt, p_decay, d_skip)
    row_slot, owners = slot_layout(pack_list[0], resp_len, resp_prompt, r_x.shape[0])
    gathered_piece = lax.all_gather(own_seed[None], "grp", axis=0, tiled=True)
    chosen = (owners[:, None] == jnp.arange(gathered_piece.shape[0])[None, :]).astype(jnp.bfloat16)
    slot_seeds = product("km,mhnp->khnp", chosen, gathered_piece).astype(jnp.bfloat16)
    skip_block = lax.dynamic_slice_in_dim(
        d_skip, lax.axis_index("seq") * block_heads, block_heads, 0
    )
    r_out = response_part(skip_block, r_x, r_bc, r_dt, r_decay, row_slot, slot_seeds)
    return (p_out, r_out)


def solution(mesh):
    placed = (
        P("grp", "seq", None),
        P("grp", "seq", None),
        P("grp", None, "seq"),
        P("grp", None, "seq"),
        P("grp", "seq"),
        P("grp", None),
        P("seq", "grp"),
        P("seq", "grp"),
        P("grp", None),
        P(),
        P(),
        P(),
    )
    return jax.shard_map(
        on_device,
        mesh=mesh,
        in_specs=placed,
        out_specs=(P("grp", "seq", None), P("grp", "seq")),
        check_vma=False,
    )
```

time: 668 us -> 257 us (0.38)
  waiting for transfers between devices: 408 us -> 112 us
  other arithmetic: 93.6 us -> 46.2 us
  local copies, waits for them, and re-layouts: 74.4 us -> 29.8 us
  blocking collectives: 34.2 us -> 0 us
  loops' own time: 21.4 us -> 0 us
  between operations: 14.7 us -> 32.7 us
  starting transfers between devices: 0.12 us -> 14.5 us
    psum x1 -> x0, waiting for transfers between devices: 156 us -> none  [from_root(): return lax.psum(kept, axis)]
    all_gather x1 -> x0, waiting for transfers between devices: 119 us -> none  [carried_in(): pieces = jax.tree.map(lambda part: lax.all_gather(part, axis), value)]
    select_n x16 -> x0, other arithmetic: 49.9 us -> none  [the longest x15 47.5 us: turn(): jnp.where(position < mine, new, old)]
    dynamic_slice x55 -> x0, local copies, waits for them, and re-layouts: 43 us -> none  [the longest x30 28.5 us: turn(): longer = join(total, jax.tree.map(lambda part: part[position], pieces))]
    unnamed x1 -> x0, blocking collectives: 34.2 us -> none
    all_gather x1, waiting for transfers between devices: 134 us -> 105 us  [on_device(): gathered_piece = lax.all_gather(own_seed[None], 'grp', axis=0, tiled=True)]
    another operation x2 -> x0, loops' own time: 21.4 us -> none  [the longest x1 21 us: response_layer(): final_pair, outputs = lax.scan(advance, initial, sliced)]
    unnamed x2 -> x20, other arithmetic: 0.01 us -> 15 us
  transfers between devices with their start and end apart: 3 -> 3, of which waited for: 3 -> 2; matrix products, arithmetic and copies ran while one was open for 1% -> 28% of each run, Pallas kernels for 0% -> 0%
where the time goes in v1:
time: 257 us; the launch traced here: 255 us
  waiting for transfers between devices  112 us (44%)
  other arithmetic  46.2 us (18%)
  between operations  32.7 us (13%)
  local copies, waits for them, and re-layouts  29.8 us (12%)
  matrix products  19.7 us (8%)
  starting transfers between devices  14.5 us (6%)
    all_gather x1, waiting for transfers between devices, on_device(): gathered_piece = lax.all_gather(own_seed[None], 'grp', axis=0, tiled=True)  105 us
    dot_general x7, matrix products, product(): jnp.einsum(einsum_form, left_side, right_side, preferred_element_type=jnp...  15.5 us
    unnamed x20, other arithmetic  15 us
    unnamed x119, local copies, waits for them, and re-layouts  10.8 us
    all_to_all x1, starting transfers between devices, prompt_part(): arrived = lax.all_to_all(payload, 'seq', 0, 0, tiled=True)  7.7 us
    mul x1, other arithmetic, response_part(): c_rows[:, :, None, :] * hot_rows[:, :, :, None]  7.35 us
    mul x1, local copies, waits for them, and re-layouts, response_part(): c_rows[:, :, None, :] * hot_rows[:, :, :, None]  7.32 us
    all_to_all x1, waiting for transfers between devices, prompt_part(): prefix = lax.all_to_all(sent_back, 'seq', 0, 0, tiled=True)  7.1 us
  transfers between devices with their start and end apart: 3, of which 2 were waited for; matrix products, arithmetic and copies ran while one was open for 28% of the time, Pallas kernels for 0%

profile of v1, /device:TPU:1, one launch (start us, length us, event | category | flops | bytes accessed | tf_op | source)
XLA Modules:
  0.0 255.2 jit_solution(14583786693908182044)
XLA Ops:
  11.8 1.4 exponential_bitcast_fusion
  13.4 1.5 copy.130
  15.9 1.4 fusion.10
  17.5 1.6 pad_maximum_fusion
  19.0 7.7 %all-to-all-start = ((f32[16,2,136,64]{2,3,1,0:T(8,128)}), f32[16,2,136,64]{2,3,1,0:T(8,128)S(1)}, u32[]{:S(2)}, u32[]{:S(2)}) async-start(f32[16,2,136,64]{2,3,1,0:T(8,128)} %bitcast.5), calls=%async_computation | async-start | bytes 4194304 | tf_op jit(solution)/shard_map/all_to_all | solution.py:66
  33.8 1.8 iota_compare_fusion.9
  40.5 1.8 iota_compare_fusion.7
  47.3 1.8 iota_compare_fusion.5
  51.3 3.2 %reshape.490 = bf16[8,256,2,64]{3,2,1,0:T(2,128)(2,1)} reshape(bf16[2048,128]{1,0:T(8,128)(2,1)} %param.16) | data formatting | bytes 1048576 | tf_op jit(solution)/shard_map/vmap()/reshape;reshape | solution.py:17
  54.5 3.5 %copy.139 = bf16[8,256,2,64]{1,3,2,0:T(8,128)(2,1)} copy(bf16[8,256,2,64]{3,2,1,0:T(2,128)(2,1)} %reshape.490) | data formatting | bytes 1048576 | tf_op jit(solution)/shard_map/vmap()/reshape;reshape | solution.py:17
  58.0 1.4 fusion.79
  65.1 1.5 compare_and_fusion
  68.0 7.3 %broadcast_multiply_fusion = bf16[8,256,8,128]{3,2,1,0:T(8,128)(2,1)} fusion(bf16[8,256,8]{2,1,0:T(8,128)(2,1)} %fusion.41, bf16[8,256,128]{2,1,0:T(8,128)(2,1)} %get-tuple-element.68), kind=kLoop, calls=%fused_computation.23 | loop fusion | flops 2097152 | bytes 4751360 | tf_op jit(solution)/shard_map/mul | solution.py:123
  75.3 7.3 %reshape.486 = bf16[8,256,1024,1]{2,1,0,3:T(8,128)(2,1)} reshape(bf16[8,256,8,128]{3,2,1,0:T(8,128)(2,1)} %broadcast_multiply_fusion) | data formatting | bytes 8388608 | tf_op jit(solution)/shard_map/mul | solution.py:123
  86.9 3.0 %fusion.38 = f32[8,2,128,64]{2,3,1,0:T(8,128)} fusion(bf16[8,256,2,64]{1,3,2,0:T(8,128)(2,1)} %copy.139, f32[8,256,128]{2,1,0:T(8,128)} %get-tuple-element.69, f32[8,2,256]{2,1,0:T(2,128)S(1)} %copy.143), kind=kOutput, calls=%fused_computation.50 | convolution fusion | flops 68157440 | bytes 2113536 | tf_op jit(solution)/shard_map/vmap(hjn,jhp->hnp)/dot_general | solution.py:10
  91.5 1.3 constant_dynamic-update-slice_fusion.14
  92.7 1.5 constant_dynamic-update-slice_fusion.13
  94.2 1.5 constant_dynamic-update-slice_fusion.12
  98.2 1.3 constant_dynamic-update-slice_fusion.8
  102.1 1.3 constant_dynamic-update-slice_fusion.4
  104.0 1.3 constant_dynamic-update-slice_fusion.2
  105.9 1.4 constant_dynamic-update-slice_fusion
  107.3 6.8 %all-to-all-start.1 = ((bf16[16,2,128,64]{2,3,1,0:T(8,128)(2,1)}), bf16[16,2,128,64]{2,3,1,0:T(8,128)(2,1)S(1)}, u32[]{:S(2)}, u32[]{:S(2)}) async-start(bf16[16,2,128,64]{2,3,1,0:T(8,128)(2,1)} %constant_dynamic-update-slice_fusion), calls=%async_computation.1 | async-start | bytes 1048576 | tf_op jit(solution)/shard_map/all_to_all | solution.py:76
  114.1 1.8 fusion.50
  115.9 7.1 %all-to-all-done.1 = bf16[16,2,128,64]{2,3,1,0:T(8,128)(2,1)S(1)} async-done(((bf16[16,2,128,64]{2,3,1,0:T(8,128)(2,1)}), bf16[16,2,128,64]{2,3,1,0:T(8,128)(2,1)S(1)}, u32[]{:S(2)}, u32[]{:S(2)}) %all-to-all-start.1) | async-done | bytes 524320 | tf_op jit(solution)/shard_map/all_to_all | solution.py:76
  123.8 1.6 fusion.60
  125.5 3.8 %fusion.13 = bf16[256,32,64]{0,2,1:T(8,128)(2,1)} fusion(f32[32,64,256]{2,1,0:T(8,128)S(1)} %fusion.60, bf16[256,32,64]{0,2,1:T(8,128)(2,1)S(1)} %bitcast.216, f32[256,256]{1,0:T(8,128)S(1)} %copy-done.14, f32[32,256]{1,0:T(8,128)S(1)} %bitcast.228, f32[32,256]{1,0:T(8,128)S(1)} %copy-done.16, pred[256,256]{1,0:T(8,128)(4,1)S(1)} %copy-done.13, ...), kind=kOutput, calls=%fused_computation.20 | convolution fusion | flops 282066944 | bytes 4620416 | tf_op jit(solution)/shard_map/hij,jhp->ihp/dot_general | solution.py:10
  129.3 2.3 copy.147
  131.6 105.2 %all-gather.2.cloned.1.call-done = bf16[64,2,128,64]{2,3,1,0:T(8,128)(2,1)} async-done(((bf16[1,2,128,64]{2,3,1,0:T(8,128)(2,1)}), bf16[64,2,128,64]{2,3,1,0:T(8,128)(2,1)}) %all-gather.2.cloned.1.call-update) | async-done | bytes 2097168 | tf_op jit(solution)/shard_map/all_gather | solution.py:148
  236.9 3.8 %fusion.48 = (f32[2,128,64]{1,2,0:T(8,128)S(1)}, f32[2,128,64]{1,2,0:T(8,128)S(1)}, f32[2,128,64]{1,2,0:T(8,128)S(1)}, f32[2,128,64]{1,2,0:T(8,128)S(1)}, f32[2,...) fusion(pred[8]{0:T(512)(128)(4,1)S(1)} %copy-done.46, ...), kind=kOutput, calls=%fused_computation.62 | convolution fusion | flops 18760192 | bytes 2818136 | tf_op jit(solution)/shard_map/km,mhnp->khnp/dot_general | solution.py:10
  243.0 1.6 fusion.28
  244.7 1.5 fusion.34
  (185 shorter events, 31.4 us)
Async XLA Ops:
  7.2 7.8 %copy-start.9 = (bf16[1,256,256]{2,1,0:T(8,128)(2,1)S(1)}, bf16[1,256,256]{2,1,0:T(8,128)(2,1)}, u32[]{:S(2)}) copy-start(bf16[1,256,256]{2,1,0:T(8,128)(2,1)} %param.13) | copy-start | bytes 393220
  19.0 7.8 %copy-start.39 = (s32[384]{0:T(512)S(1)}, s32[384]{0:T(512)}, u32[]{:S(2)}) copy-start(s32[384]{0:T(512)} %param.22) | copy-start | bytes 4612
  19.0 7.8 %copy-start.40 = (s32[384]{0:T(512)S(1)}, s32[384]{0:T(512)}, u32[]{:S(2)}) copy-start(s32[384]{0:T(512)} %param.21) | copy-start | bytes 4612
  19.0 7.8 %copy-start.48 = (s32[1,8]{1,0:T(1,128)S(1)}, s32[1,8]{1,0:T(1,128)}, u32[]{:S(2)}) copy-start(s32[1,8]{1,0:T(1,128)} %param.20) | copy-start | bytes 100
  19.0 70.9 %all-to-all-start = ((f32[16,2,136,64]{2,3,1,0:T(8,128)}), f32[16,2,136,64]{2,3,1,0:T(8,128)S(1)}, u32[]{:S(2)}, u32[]{:S(2)}) async-start(f32[16,2,136,64]{2,3,1,0:T(8,128)} %bitcast.5), calls=%async_computation | async-start | bytes 4194304 | tf_op jit(solution)/shard_map/all_to_all | solution.py:66
  26.8 31.2 %copy-start.1 = (bf16[2048,256]{1,0:T(8,128)(2,1)S(1)}, bf16[2048,256]{1,0:T(8,128)(2,1)}, u32[]{:S(2)}) copy-start(bf16[2048,256]{1,0:T(8,128)(2,1)} %param.17) | copy-start | bytes 3145732
  26.8 210.0 %all-gather.2.cloned.1.call-start = ((), (), s32[]{:S(2)}) async-start(), calls=%async_computation.2 | async-start | bytes 2129920 | tf_op jit(solution)/shard_map/all_gather | solution.py:148
  26.8 38.3 %copy-start.12 = (pred[256,256]{1,0:T(8,128)(4,1)}, pred[256,256]{1,0:T(8,128)(4,1)S(1)}, u32[]{:S(2)}) copy-start(pred[256,256]{1,0:T(8,128)(4,1)S(1)} %iota_compare_fusion.1) | copy-start | bytes 196612
  54.5 4.9 %copy-start.17 = (f32[2,2048]{1,0:T(2,128)S(1)}, f32[2,2048]{1,0:T(2,128)}, u32[]{:S(2)}) copy-start(f32[2,2048]{1,0:T(2,128)} %param.19) | copy-start | bytes 49156
  54.5 9.6 %copy-start.18 = (f32[2,2048]{1,0:T(2,128)S(1)}, f32[2,2048]{1,0:T(2,128)}, u32[]{:S(2)}) copy-start(f32[2,2048]{1,0:T(2,128)} %param.18) | copy-start | bytes 49156
  75.3 7.9 %copy-start.51 = (f32[32]{0:T(128)S(1)}, f32[32]{0:T(128)}, u32[]{:S(2)}) copy-start(f32[32]{0:T(128)} %param.23) | copy-start | bytes 388
  97.6 16.4 %copy-start.49 = (s32[1,8]{1,0:T(1,128)S(1)}, s32[1,8]{1,0:T(1,128)}, u32[]{:S(2)}) copy-start(s32[1,8]{1,0:T(1,128)} %param.20) | copy-start | bytes 100
  97.6 16.5 %copy-start.50 = (s32[8]{0:T(128)S(1)}, s32[8]{0:T(128)}, u32[]{:S(2)}) copy-start(s32[8]{0:T(128)} %get-tuple-element.44) | copy-start | bytes 100
  107.3 16.5 %copy-start.10 = (bf16[1,256,256]{2,1,0:T(8,128)(2,1)S(1)}, bf16[1,256,256]{2,1,0:T(8,128)(2,1)}, u32[]{:S(2)}) copy-start(bf16[1,256,256]{2,1,0:T(8,128)(2,1)} %param.13) | copy-start | bytes 393220
  107.3 15.7 %all-to-all-start.1 = ((bf16[16,2,128,64]{2,3,1,0:T(8,128)(2,1)}), bf16[16,2,128,64]{2,3,1,0:T(8,128)(2,1)S(1)}, u32[]{:S(2)}, u32[]{:S(2)}) async-start(bf16[16,2,128,64]{2,3,1,0:T(8,128)(2,1)} %constant_dynamic-update-slice_fusion), calls=%async_computation.1 | async-start | bytes 1048576 | tf_op jit(solution)/shard_map/all_to_all | solution.py:76
  115.9 9.5 %copy-start.13 = (pred[256,256]{1,0:T(8,128)(4,1)S(1)}, pred[256,256]{1,0:T(8,128)(4,1)}, u32[]{:S(2)}) copy-start(pred[256,256]{1,0:T(8,128)(4,1)} %copy-done.12) | copy-start | bytes 196612
  115.9 9.5 %copy-start.16 = (f32[32,256]{1,0:T(8,128)S(1)}, f32[32,256]{1,0:T(8,128)}, u32[]{:S(2)}) copy-start(f32[32,256]{1,0:T(8,128)} %copy-done.15) | copy-start | bytes 98308
  115.9 9.5 %copy-start.20 = (f32[1,32,256]{2,1,0:T(8,128)S(1)}, f32[1,32,256]{2,1,0:T(8,128)}, u32[]{:S(2)}) copy-start(f32[1,32,256]{2,1,0:T(8,128)} %param.14) | copy-start | bytes 98308
  115.9 9.5 %copy-start.21 = (f32[256,32]{0,1:T(8,128)S(1)}, f32[256,32]{0,1:T(8,128)}, u32[]{:S(2)}) copy-start(f32[256,32]{0,1:T(8,128)} %get-tuple-element.66) | copy-start | bytes 98308
  115.9 9.5 %copy-start.52 = (f32[32]{0:T(128)S(1)}, f32[32]{0:T(128)}, u32[]{:S(2)}) copy-start(f32[32]{0:T(128)} %param.23) | copy-start | bytes 388
  129.3 107.5 %copy-start.42 = (pred[8]{0:T(512)(128)(4,1)S(1)}, pred[8]{0:T(512)(128)(4,1)}, u32[]{:S(2)}) copy-start(pred[8]{0:T(512)(128)(4,1)} %get-tuple-element.99) | copy-start | bytes 28
  129.3 107.5 %copy-start.43 = (pred[8]{0:T(512)(128)(4,1)S(1)}, pred[8]{0:T(512)(128)(4,1)}, u32[]{:S(2)}) copy-start(pred[8]{0:T(512)(128)(4,1)} %get-tuple-element.100) | copy-start | bytes 28
  129.3 107.5 %copy-start.44 = (pred[8]{0:T(512)(128)(4,1)S(1)}, pred[8]{0:T(512)(128)(4,1)}, u32[]{:S(2)}) copy-start(pred[8]{0:T(512)(128)(4,1)} %get-tuple-element.97) | copy-start | bytes 28
  129.3 107.5 %copy-start.45 = (pred[8]{0:T(512)(128)(4,1)S(1)}, pred[8]{0:T(512)(128)(4,1)}, u32[]{:S(2)}) copy-start(pred[8]{0:T(512)(128)(4,1)} %get-tuple-element.98) | copy-start | bytes 28
  129.3 107.5 %copy-start.46 = (pred[8]{0:T(512)(128)(4,1)S(1)}, pred[8]{0:T(512)(128)(4,1)}, u32[]{:S(2)}) copy-start(pred[8]{0:T(512)(128)(4,1)} %get-tuple-element.95) | copy-start | bytes 28
  129.3 107.5 %copy-start.47 = (pred[8]{0:T(512)(128)(4,1)S(1)}, pred[8]{0:T(512)(128)(4,1)}, u32[]{:S(2)}) copy-start(pred[8]{0:T(512)(128)(4,1)} %get-tuple-element.96) | copy-start | bytes 28
  129.3 107.5 %copy-start.54 = (pred[8]{0:T(512)(128)(4,1)S(1)}, pred[8]{0:T(512)(128)(4,1)}, u32[]{:S(2)}) copy-start(pred[8]{0:T(512)(128)(4,1)} %iota_compare_fusion.11) | copy-start | bytes 28
  236.8 4.1 %copy-start.37 = (f32[2]{0:T(128)S(1)}, f32[2]{0:T(128)}, u32[]{:S(2)}) copy-start(f32[2]{0:T(128)} %get-tuple-element.41) | copy-start | bytes 28
  236.9 4.2 %copy-start.36 = (f32[2]{0:T(128)S(1)}, f32[2]{0:T(128)}, u32[]{:S(2)}) copy-start(f32[2]{0:T(128)} %get-tuple-element.40) | copy-start | bytes 28
  236.9 4.3 %copy-start.35 = (f32[2]{0:T(128)S(1)}, f32[2]{0:T(128)}, u32[]{:S(2)}) copy-start(f32[2]{0:T(128)} %get-tuple-element.39) | copy-start | bytes 28
  236.9 4.4 %copy-start.34 = (f32[2]{0:T(128)S(1)}, f32[2]{0:T(128)}, u32[]{:S(2)}) copy-start(f32[2]{0:T(128)} %get-tuple-element.38) | copy-start | bytes 28
  236.9 4.5 %copy-start.33 = (f32[2]{0:T(128)S(1)}, f32[2]{0:T(128)}, u32[]{:S(2)}) copy-start(f32[2]{0:T(128)} %get-tuple-element.37) | copy-start | bytes 28
  (26 other events, 47.7 us)
Sparse Core Ops, SparseCore 0:
  91.6 145.1 all-gather.1

commit v2 on v1

--- a/solution.py
+++ b/solution.py
@@ -58,21 +58,23 @@
         p_x[0], p_bc[0], p_dt[0], p_decay[0], jnp.zeros((STRETCH,), jnp.int32)
     )
     channels = inputs.shape[2]
-    block_gain = jnp.exp(gained[:, -1])
+    block_gain = gained[:, -1]
     pad = 8
     gain_rows = jnp.broadcast_to(block_gain[:, None, None], (head_count, pad, channels))
     payload = jnp.concatenate([local_state, gain_rows], axis=1)
     payload = payload.reshape(groups, block_heads, state_width + pad, channels)
     arrived = lax.all_to_all(payload, "seq", 0, 0, tiled=True)
     pieces = arrived[:, :, :state_width, :]
-    gains = arrived[:, :, state_width, 0]
-    state = jnp.zeros((block_heads, state_width, channels), jnp.float32)
-    prefixes = []
-    for position in range(groups):
-        prefixes.append(state.astype(jnp.bfloat16))
-        state = gains[position][:, None, None] * state + pieces[position]
-    own_seed = state.astype(jnp.bfloat16)
-    sent_back = jnp.stack(prefixes, axis=0)
+    log_gains = arrived[:, :, state_width, 0]
+    ends = jnp.arange(groups + 1)[:, None, None]
+    sources = jnp.arange(groups)[None, :, None]
+    between = jnp.arange(groups)[None, None, :]
+    spans = (sources < between) & (between < ends)
+    exponents = jnp.sum(jnp.where(spans[..., None], log_gains[None, None], 0.0), axis=2)
+    weights = jnp.where(sources < ends, jnp.exp(exponents), 0.0)
+    states = jnp.sum(weights[:, :, :, None, None] * pieces[None], axis=1)
+    own_seed = states[groups].astype(jnp.bfloat16)
+    sent_back = states[:groups].astype(jnp.bfloat16)
     prefix = lax.all_to_all(sent_back, "seq", 0, 0, tiled=True)
     prefix = prefix.reshape(head_count, state_width, channels)
     carried = product("in,hnp->ihp", c_rows, prefix) * jnp.exp(gained).T[:, :, None]
@@ -144,6 +146,9 @@
     groups = lax.axis_size("seq")
     block_heads = head_count // groups
     p_out, own_seed = prompt_part(p_x, p_bc, p_dt, p_decay, d_skip)
+    own_seed, r_x, r_bc, r_dt, r_decay = lax.optimization_barrier(
+        (own_seed, r_x, r_bc, r_dt, r_decay)
+    )
     row_slot, owners = slot_layout(pack_list[0], resp_len, resp_prompt, r_x.shape[0])
     gathered_piece = lax.all_gather(own_seed[None], "grp", axis=0, tiled=True)
     chosen = (owners[:, None] == jnp.arange(gathered_piece.shape[0])[None, :]).astype(jnp.bfloat16)

time: 257 us -> 227 us (0.88)
  other arithmetic: 46.2 us -> 31.2 us
  local copies, waits for them, and re-layouts: 29.8 us -> 22.8 us
  waiting for transfers between devices: 112 us -> 105 us
    unnamed x20 -> x6, other arithmetic: 15 us -> 0.57 us
    all_to_all x1, waiting for transfers between devices: 7.1 us -> 0.01 us  [prompt_part(): prefix = lax.all_to_all(sent_back, 'seq', 0, 0, tiled=True)]
    another operation x2, local copies, waits for them, and re-layouts: 6.66 us -> 1.03 us  [block_terms(): inputs = block_x.reshape(length, head_count, -1)]
    unnamed x119 -> x64, local copies, waits for them, and re-layouts: 10.8 us -> 8.22 us
    dot_general x7 -> x6, matrix products: 15.5 us -> 15.8 us  [product(): jnp.einsum(einsum_form, left_side, right_side, preferred_element_type=jnp...]
  transfers between devices with their start and end apart: 3 -> 3, of which waited for: 2 -> 1; matrix products, arithmetic and copies ran while one was open for 28% -> 20% of each run, Pallas kernels for 0% -> 0%
where the time goes in v2:
time: 227 us; the launch traced here: 226 us
  waiting for transfers between devices  105 us (46%)
  between operations  33.2 us (15%)
  other arithmetic  31.2 us (14%)
  local copies, waits for them, and re-layouts  22.8 us (10%)
  matrix products  19 us (8%)
  starting transfers between devices  14.3 us (6%)
    all_gather x1, waiting for transfers between devices, on_device(): gathered_piece = lax.all_gather(own_seed[None], 'grp', axis=0, tiled=True)  105 us
    dot_general x6, matrix products, product(): jnp.einsum(einsum_form, left_side, right_side, preferred_element_type=jnp...  15.8 us
    unnamed x64, local copies, waits for them, and re-layouts  8.22 us
    all_to_all x1, starting transfers between devices, prompt_part(): arrived = lax.all_to_all(payload, 'seq', 0, 0, tiled=True)  7.58 us
    mul x1, local copies, waits for them, and re-layouts, response_part(): c_rows[:, :, None, :] * hot_rows[:, :, :, None]  7.32 us
    all_to_all x1, starting transfers between devices, prompt_part(): prefix = lax.all_to_all(sent_back, 'seq', 0, 0, tiled=True)  6.72 us
    eq x4, other arithmetic, response_part(): slot_ids == final_slot  6.64 us
    mul x1, other arithmetic, response_part(): c_rows[:, :, None, :] * hot_rows[:, :, :, None]  5.93 us
  transfers between devices with their start and end apart: 3, of which 1 were waited for; matrix products, arithmetic and copies ran while one was open for 20% of the time, Pallas kernels for 0%

profile of v2, /device:TPU:1, one launch (start us, length us, event | category | flops | bytes accessed | tf_op | source)
XLA Modules:
  0.0 225.9 jit_solution(8151779107403502980)
XLA Ops:
  8.8 0.8 bitcast_subtract_fusion
  10.5 1.2 select_reduce_fusion
  11.8 1.4 exponential_bitcast_fusion
  13.4 1.5 copy.114
  14.9 0.9 slice_convert_fusion.1
  15.8 1.4 fusion.10
  17.4 1.6 pad_maximum_fusion
  19.0 7.6 %all-to-all-start = ((f32[16,2,136,64]{2,3,1,0:T(8,128)}), f32[16,2,136,64]{2,3,1,0:T(8,128)S(1)}, u32[]{:S(2)}, u32[]{:S(2)}) async-start(f32[16,2,136,64]{2,3,1,0:T(8,128)} %bitcast.5), calls=%async_computation | async-start | bytes 4194304 | tf_op jit(solution)/shard_map/all_to_all | solution.py:66
  29.3 1.9 iota_compare_fusion.7
  31.2 1.7 iota_compare_fusion.11
  32.9 1.8 iota_compare_fusion.9
  34.7 1.2 iota_compare_fusion.13
  56.3 1.5 compare_and_fusion
  58.5 2.1 multiply_reduce_fusion
  61.3 0.9 fusion.60
  62.2 0.8 slice.218
  63.0 6.7 %all-to-all-start.1 = ((bf16[16,2,128,64]{2,3,1,0:T(8,128)(2,1)}), bf16[16,2,128,64]{2,3,1,0:T(8,128)(2,1)}, u32[]{:S(2)}, u32[]{:S(2)}) async-start(bf16[16,2,128,64]{2,3,1,0:T(8,128)(2,1)} %slice.218), calls=%async_computation.1 | async-start | bytes 1048576 | tf_op jit(solution)/shard_map/all_to_all | solution.py:78
  70.9 1.2 reduce-window.31
  72.5 0.8 fusion.65
  73.3 1.8 select_reduce_fusion.1
  75.9 1.6 fusion.38
  77.5 5.9 %broadcast_multiply_fusion = bf16[8,256,8,128]{3,2,1,0:T(8,128)(2,1)} fusion(bf16[8,256,8]{2,1,0:T(8,128)(2,1)S(1)} %fusion.41, bf16[8,256,128]{2,1,0:T(8,128)(2,1)S(1)} %get-tuple-element.54), kind=kLoop, calls=%fused_computation.24 | loop fusion | flops 2097152 | bytes 4751360 | tf_op jit(solution)/shard_map/mul | solution.py:125
  83.6 7.3 %reshape.482 = bf16[8,256,1024,1]{2,1,0,3:T(8,128)(2,1)} reshape(bf16[8,256,8,128]{3,2,1,0:T(8,128)(2,1)} %broadcast_multiply_fusion) | data formatting | bytes 8388608 | tf_op jit(solution)/shard_map/mul | solution.py:125
  92.1 1.5 fusion.58
  93.6 5.2 %fusion.13 = bf16[256,32,64]{0,2,1:T(8,128)(2,1)} fusion(f32[32,64,256]{2,1,0:T(8,128)S(1)} %fusion.58, bf16[256,32,64]{0,2,1:T(8,128)(2,1)} %bitcast.217, f32[256,256]{1,0:T(8,128)} %fusion.60, f32[32,256]{1,0:T(8,128)S(1)} %bitcast.230, f32[32,256]{1,0:T(8,128)S(1)} %copy_bitcast_fusion.1, pred[256,256]{1,0:T(8,128)(4,1)S(1)} %iota_compare_fusion.1, ...), kind=kOutput, calls=%fused_computation.21 | convolution fusion | flops 282066944 | bytes 4620416 | tf_op jit(solution)/shard_map/hij,jhp->ihp/dot_general | solution.py:10
  98.8 2.3 %copy.133 = bf16[1,256,2048]{2,1,0:T(8,128)(2,1)} copy(bf16[1,256,2048]{1,2,0:T(8,128)(2,1)} %bitcast.218) | data formatting | bytes 2097152
  101.1 105.4 %all-gather.3.cloned.1.call-done = bf16[128,128,64]{1,2,0:T(8,128)(2,1)} async-done(((bf16[2,128,64]{1,2,0:T(8,128)(2,1)}), bf16[128,128,64]{1,2,0:T(8,128)(2,1)}) %all-gather.3.cloned.1.call-update) | async-done | bytes 2097168 | tf_op jit(solution)/shard_map/all_gather | solution.py:153
  206.6 3.9 %fusion.48 = (f32[2,128,64]{1,2,0:T(8,128)S(1)}, f32[2,128,64]{1,2,0:T(8,128)S(1)}, f32[2,128,64]{1,2,0:T(8,128)S(1)}, f32[2,128,64]{1,2,0:T(8,128)S(1)}, f32[2,...) fusion(pred[8]{0:T(512)(128)(4,1)} %get-tuple-element.81, ...), kind=kOutput, calls=%fused_computation.62 | convolution fusion | flops 18760192 | bytes 2818136 | tf_op jit(solution)/shard_map/km,mhnp->khnp/dot_general | solution.py:10
  211.6 1.5 fusion.28
  213.2 2.3 %fusion.34 = bf16[8,256,2,64]{1,3,2,0:T(8,128)(2,1)} fusion(f32[8,256,2,64]{1,3,2,0:T(8,128)S(1)} %fusion.28, bf16[8,256,2,64]{1,3,2,0:T(8,128)(2,1)S(1)} %copy-done.3, f32[8,256,256]{2,1,0:T(8,128)S(1)} %fusion.49, f32[8,2,256]{2,1,0:T(2,128)S(1)} %copy.124, f32[8,2,256]{2,1,0:T(2,128)S(1)} %copy-done.14, pred[8,256,256]{2,1,0:T(8,128)(4,1)S(1)} %copy-done.7, ...), kind=kOutput, calls=%fused_computation.48 | convolution fusion | flops 141033472 | bytes 4753416 | tf_op jit(solution)/shard_map/vmap(hij,jhp->ihp)/dot_general | solution.py:10
  215.5 2.4 %copy.137 = bf16[8,256,2,64]{3,2,1,0:T(2,128)(2,1)S(1)} copy(bf16[8,256,2,64]{1,3,2,0:T(8,128)(2,1)} %fusion.34) | data formatting | bytes 1048576
  217.8 1.3 reshape.485
  (125 shorter events, 13.2 us)
Async XLA Ops:
  14.9 4.1 %copy-start.5 = (bf16[1,256,2048]{1,2,0:T(8,128)(2,1)}, bf16[1,256,2048]{1,2,0:T(8,128)(2,1)S(1)}, u32[]{:S(2)}) copy-start(bf16[1,256,2048]{1,2,0:T(8,128)(2,1)S(1)} %copy.114) | copy-start | bytes 3145732
  17.4 9.9 %copy-start.21 = (s32[384]{0:T(512)S(1)}, s32[384]{0:T(512)}, u32[]{:S(2)}) copy-start(s32[384]{0:T(512)} %param.22) | copy-start | bytes 4612
  17.4 9.9 %copy-start.22 = (s32[384]{0:T(512)S(1)}, s32[384]{0:T(512)}, u32[]{:S(2)}) copy-start(s32[384]{0:T(512)} %param.21) | copy-start | bytes 4612
  17.4 9.9 %copy-start.24 = (s32[1,8]{1,0:T(1,128)S(1)}, s32[1,8]{1,0:T(1,128)}, u32[]{:S(2)}) copy-start(s32[1,8]{1,0:T(1,128)} %param.20) | copy-start | bytes 100
  17.4 37.1 %copy-start.25 = (f32[32]{0:T(128)S(1)}, f32[32]{0:T(128)}, u32[]{:S(2)}) copy-start(f32[32]{0:T(128)} %param.23) | copy-start | bytes 388
  19.0 38.9 %all-to-all-start = ((f32[16,2,136,64]{2,3,1,0:T(8,128)}), f32[16,2,136,64]{2,3,1,0:T(8,128)S(1)}, u32[]{:S(2)}, u32[]{:S(2)}) async-start(f32[16,2,136,64]{2,3,1,0:T(8,128)} %bitcast.5), calls=%async_computation | async-start | bytes 4194304 | tf_op jit(solution)/shard_map/all_to_all | solution.py:66
  26.6 34.7 %copy-start.8 = (bf16[1,256,256]{2,1,0:T(8,128)(2,1)S(1)}, bf16[1,256,256]{2,1,0:T(8,128)(2,1)}, u32[]{:S(2)}) copy-start(bf16[1,256,256]{2,1,0:T(8,128)(2,1)} %param.13) | copy-start | bytes 393220
  26.6 180.0 %all-gather.3.cloned.1.call-start = ((), (), s32[]{:S(2)}) async-start(), calls=%async_computation.2 | async-start | bytes 2129920 | tf_op jit(solution)/shard_map/all_gather | solution.py:153
  56.0 13.8 %copy-start.6 = (bf16[2048,128]{1,0:T(8,128)(2,1)S(1)}, bf16[2048,128]{1,0:T(8,128)(2,1)}, u32[]{:S(2)}) copy-start(bf16[2048,128]{1,0:T(8,128)(2,1)} %param.16) | copy-start | bytes 1572868
  58.5 12.4 %copy-start.10 = (f32[2,2048]{1,0:T(2,128)S(1)}, f32[2,2048]{1,0:T(2,128)}, u32[]{:S(2)}) copy-start(f32[2,2048]{1,0:T(2,128)} %param.19) | copy-start | bytes 49156
  58.5 17.3 %copy-start.1 = (bf16[2048,256]{1,0:T(8,128)(2,1)S(1)}, bf16[2048,256]{1,0:T(8,128)(2,1)}, u32[]{:S(2)}) copy-start(bf16[2048,256]{1,0:T(8,128)(2,1)} %param.17) | copy-start | bytes 3145732
  63.0 29.1 %all-to-all-start.1 = ((bf16[16,2,128,64]{2,3,1,0:T(8,128)(2,1)}), bf16[16,2,128,64]{2,3,1,0:T(8,128)(2,1)}, u32[]{:S(2)}, u32[]{:S(2)}) async-start(bf16[16,2,128,64]{2,3,1,0:T(8,128)(2,1)} %slice.218), calls=%async_computation.1 | async-start | bytes 1048576 | tf_op jit(solution)/shard_map/all_to_all | solution.py:78
  70.8 12.6 %copy-start.2 = (bf16[8,256,2,64]{1,3,2,0:T(8,128)(2,1)}, bf16[8,256,2,64]{1,3,2,0:T(8,128)(2,1)S(1)}, u32[]{:S(2)}) copy-start(bf16[8,256,2,64]{1,3,2,0:T(8,128)(2,1)S(1)} %copy.125) | copy-start | bytes 1572868
  75.9 7.6 %copy-start.11 = (f32[2,2048]{1,0:T(2,128)S(1)}, f32[2,2048]{1,0:T(2,128)}, u32[]{:S(2)}) copy-start(f32[2,2048]{1,0:T(2,128)} %param.18) | copy-start | bytes 49156
  90.9 2.7 %copy-start.12 = (f32[1,32,256]{2,1,0:T(8,128)S(1)}, f32[1,32,256]{2,1,0:T(8,128)}, u32[]{:S(2)}) copy-start(f32[1,32,256]{2,1,0:T(8,128)} %param.14) | copy-start | bytes 98308
  90.9 2.7 %copy-start.13 = (f32[256,32]{0,1:T(8,128)S(1)}, f32[256,32]{0,1:T(8,128)}, u32[]{:S(2)}) copy-start(f32[256,32]{0,1:T(8,128)} %get-tuple-element.52) | copy-start | bytes 98308
  90.9 2.7 %copy-start.26 = (f32[32]{0:T(128)S(1)}, f32[32]{0:T(128)}, u32[]{:S(2)}) copy-start(f32[32]{0:T(128)} %param.23) | copy-start | bytes 388
  98.8 111.6 %copy-start.9 = (bf16[8,2,128,64]{2,3,1,0:T(8,128)(2,1)S(1)}, bf16[8,2,128,64]{2,3,1,0:T(8,128)(2,1)}, u32[]{:S(2)}) copy-start(bf16[8,2,128,64]{2,3,1,0:T(8,128)(2,1)} %constant_dynamic-update-slice_fusion) | copy-start | bytes 786436
  98.8 111.8 %copy-start.20 = (f32[2]{0:T(128)S(1)}, f32[2]{0:T(128)}, u32[]{:S(2)}) copy-start(f32[2]{0:T(128)} %get-tuple-element.36) | copy-start | bytes 28
  98.8 111.9 %copy-start.19 = (f32[2]{0:T(128)S(1)}, f32[2]{0:T(128)}, u32[]{:S(2)}) copy-start(f32[2]{0:T(128)} %get-tuple-element.35) | copy-start | bytes 28
  98.8 112.0 %copy-start.18 = (f32[2]{0:T(128)S(1)}, f32[2]{0:T(128)}, u32[]{:S(2)}) copy-start(f32[2]{0:T(128)} %get-tuple-element.34) | copy-start | bytes 28
  98.8 112.1 %copy-start.17 = (f32[2]{0:T(128)S(1)}, f32[2]{0:T(128)}, u32[]{:S(2)}) copy-start(f32[2]{0:T(128)} %get-tuple-element.33) | copy-start | bytes 28
  98.8 112.1 %copy-start.16 = (f32[2]{0:T(128)S(1)}, f32[2]{0:T(128)}, u32[]{:S(2)}) copy-start(f32[2]{0:T(128)} %get-tuple-element.32) | copy-start | bytes 28
  98.8 112.2 %copy-start.15 = (f32[2]{0:T(128)S(1)}, f32[2]{0:T(128)}, u32[]{:S(2)}) copy-start(f32[2]{0:T(128)} %get-tuple-element.31) | copy-start | bytes 28
  206.5 3.9 %copy-start.4 = (f32[8,2,128,64]{2,3,1,0:T(8,128)S(1)}, f32[8,2,128,64]{2,3,1,0:T(8,128)}, u32[]{:S(2)}) copy-start(f32[8,2,128,64]{2,3,1,0:T(8,128)} %fusion.38) | copy-start | bytes 1572868
  206.5 5.0 %copy-start = (bf16[8,256,1024,1]{2,1,0,3:T(8,128)(2,1)S(1)}, bf16[8,256,1024,1]{2,1,0,3:T(8,128)(2,1)}, u32[]{:S(2)}) copy-start(bf16[8,256,1024,1]{2,1,0,3:T(8,128)(2,1)} %reshape.482) | copy-start | bytes 12582916
  211.5 1.6 copy-start.3
  211.5 1.6 copy-start.7
  211.5 1.6 copy-start.14
  211.6 1.6 copy-start.23
  211.6 1.6 copy-start.27
Sparse Core Ops, SparseCore 0:
  61.4 145.0 all-gather.2

commit v3 on v2

--- a/solution.py
+++ b/solution.py
@@ -139,6 +139,23 @@
     return output.reshape(rows_x.shape).astype(jnp.bfloat16)
 
 
+def gather_all(piece, axis):
+    count = lax.axis_size(axis)
+    mine = lax.axis_index(axis)
+    rounds = count.bit_length() - 1
+    assert 1 << rounds == count
+    held = piece
+    for level in range(rounds):
+        step = 1 << (rounds - 1 - level)
+        pairs = [(index, index ^ step) for index in range(count)]
+        other = lax.ppermute(held, axis, pairs)
+        lower = (mine & step) == 0
+        held = jnp.stack(
+            [jnp.where(lower, held, other), jnp.where(lower, other, held)], axis=level
+        )
+    return held.reshape((count,) + piece.shape)
+
+
 def on_device(
     p_x, p_bc, p_dt, p_decay, r_x, r_bc, r_dt, r_decay, pack_list, resp_len, resp_prompt, d_skip
 ):
@@ -150,7 +167,7 @@
         (own_seed, r_x, r_bc, r_dt, r_decay)
     )
     row_slot, owners = slot_layout(pack_list[0], resp_len, resp_prompt, r_x.shape[0])
-    gathered_piece = lax.all_gather(own_seed[None], "grp", axis=0, tiled=True)
+    gathered_piece = gather_all(own_seed, "grp")
     chosen = (owners[:, None] == jnp.arange(gathered_piece.shape[0])[None, :]).astype(jnp.bfloat16)
     slot_seeds = product("km,mhnp->khnp", chosen, gathered_piece).astype(jnp.bfloat16)
     skip_block = lax.dynamic_slice_in_dim(

time: 227 us -> 199 us (0.88)
  waiting for transfers between devices: 105 us -> 34.6 us
  starting transfers between devices: 14.3 us -> 62.6 us
  between operations: 33.2 us -> 19.3 us
  other arithmetic: 31.2 us -> 36.6 us
  local copies, waits for them, and re-layouts: 22.8 us -> 26.8 us
    all_gather x1 -> x0, waiting for transfers between devices: 105 us -> none  [on_device(): gathered_piece = lax.all_gather(own_seed[None], 'grp', axis=0, tiled=True)]
    ppermute x0 -> x6, starting transfers between devices: none -> 48.3 us  [gather_all(): other = lax.ppermute(held, axis, pairs)]
    ppermute x0 -> x6, waiting for transfers between devices: none -> 34.6 us  [gather_all(): other = lax.ppermute(held, axis, pairs)]
    another operation x7 -> x19, other arithmetic: 2.15 us -> 6.53 us  [the longest x12 4.38 us: gather_all(): jnp.stack([jnp.where(lower, held, other), jnp.where(lower, other, held)],...]
    another operation x2, local copies, waits for them, and re-layouts: 1.03 us -> 4.23 us  [block_terms(): inputs = block_x.reshape(length, head_count, -1)]
    dot_general x6, matrix products: 15.8 us -> 13.2 us  [product(): jnp.einsum(einsum_form, left_side, right_side, preferred_element_type=jnp...]
    unnamed x64 -> x68, local copies, waits for them, and re-layouts: 8.22 us -> 7.44 us
  transfers between devices with their start and end apart: 3 -> 8, of which waited for: 1 -> 3; matrix products, arithmetic and copies ran while one was open for 20% -> 26% of each run, Pallas kernels for 0% -> 0%
where the time goes in v3:
time: 199 us; the launch traced here: 198 us
  starting transfers between devices  62.6 us (31%)
  other arithmetic  36.6 us (18%)
  waiting for transfers between devices  34.6 us (17%)
  local copies, waits for them, and re-layouts  26.8 us (13%)
  between operations  19.3 us (10%)
  matrix products  17.7 us (9%)
    ppermute x6, starting transfers between devices, gather_all(): other = lax.ppermute(held, axis, pairs)  48.3 us
    ppermute x6, waiting for transfers between devices, gather_all(): other = lax.ppermute(held, axis, pairs)  34.6 us
    dot_general x6, matrix products, product(): jnp.einsum(einsum_form, left_side, right_side, preferred_element_type=jnp...  13.2 us
    all_to_all x1, starting transfers between devices, prompt_part(): arrived = lax.all_to_all(payload, 'seq', 0, 0, tiled=True)  7.57 us
    mul x1, other arithmetic, response_part(): c_rows[:, :, None, :] * hot_rows[:, :, :, None]  7.48 us
    unnamed x68, local copies, waits for them, and re-layouts  7.44 us
    mul x1, local copies, waits for them, and re-layouts, response_part(): c_rows[:, :, None, :] * hot_rows[:, :, :, None]  7.37 us
    all_to_all x1, starting transfers between devices, prompt_part(): prefix = lax.all_to_all(sent_back, 'seq', 0, 0, tiled=True)  6.71 us
  transfers between devices with their start and end apart: 8, of which 3 were waited for; matrix products, arithmetic and copies ran while one was open for 26% of the time, Pallas kernels for 0%

profile of v3, /device:TPU:1, one launch (start us, length us, event | category | flops | bytes accessed | tf_op | source)
XLA Modules:
  0.0 197.5 jit_solution(3186705299111008195)
XLA Ops:
  5.2 1.4 exponential_bitcast_fusion
  6.8 2.3 %copy.115 = bf16[1,256,2048]{1,2,0:T(8,128)(2,1)} copy(bf16[1,256,2048]{2,1,0:T(8,128)(2,1)} %param.12) | data formatting | bytes 2097152 | tf_op args[0]
  10.0 2.7 %fusion.10 = f32[32,128,64]{1,2,0:T(8,128)S(1)} fusion(bf16[256,32,64]{0,2,1:T(8,128)(2,1)} %bitcast.2, f32[256,128]{1,0:T(8,128)S(1)} %slice_convert_fusion.1, f32[32,256]{1,0:T(8,128)S(1)} %get-tuple-element.70), kind=kOutput, calls=%fused_computation.16 | convolution fusion | flops 136314880 | bytes 2260992 | tf_op jit(solution)/shard_map/hjn,jhp->hnp/dot_general | solution.py:10
  12.8 1.5 pad_maximum_fusion
  14.4 7.6 %all-to-all-start = ((f32[16,2,136,64]{2,3,1,0:T(8,128)}), f32[16,2,136,64]{2,3,1,0:T(8,128)S(1)}, u32[]{:S(2)}, u32[]{:S(2)}) async-start(f32[16,2,136,64]{2,3,1,0:T(8,128)} %bitcast.5), calls=%async_computation | async-start | bytes 4194304 | tf_op jit(solution)/shard_map/all_to_all | solution.py:66
  25.3 1.7 iota_compare_fusion.11
  29.5 1.8 iota_compare_fusion.9
  33.9 1.9 iota_compare_fusion.7
  52.6 1.5 compare_and_fusion
  54.7 2.1 %multiply_reduce_fusion = bf16[17,2,128,64]{2,3,1,0:T(8,128)(2,1)S(1)} fusion(f32[16,2,128,64]{2,3,1,0:T(8,128)S(1)} %slice.217, f32[17,16,2]{2,1,0:T(8,128)S(1)} %copy.117), kind=kLoop, calls=%fused_computation | loop fusion | flops 8634368 | bytes 1607808 | tf_op jit(solution)/shard_map/reduce_sum | solution.py:75
  58.7 28.7 %collective-permute-start = (bf16[2,128,64]{1,2,0:T(8,128)(2,1)S(1)}, bf16[2,128,64]{1,2,0:T(8,128)(2,1)S(1)}, u32[]{:S(2)}, u32[]{:S(2)}) collective-permute-start(bf16[2,128,64]{1,2,0:T(8,128)(2,1)S(1)} %slice_bitcast_fusion), channel_id=1, source_target_pairs={{0,32},{1,33},{2,34},{3,35},{4,36},{5,37},{6,38},{7,39},{8,40},{9,... | collective-permute-start | bytes 98312 | tf_op jit(solution)/shard_map/ppermute | solution.py:151
  87.4 7.5 %broadcast_multiply_fusion = bf16[8,256,8,128]{3,2,1,0:T(8,128)(2,1)} fusion(bf16[8,256,8]{2,1,0:T(8,128)(2,1)} %fusion.36, bf16[8,256,128]{2,1,0:T(8,128)(2,1)S(1)} %get-tuple-element.56), kind=kLoop, calls=%fused_computation.23 | loop fusion | flops 2097152 | bytes 4751360 | tf_op jit(solution)/shard_map/mul | solution.py:125
  96.2 5.8 %collective-permute-start.1 = (bf16[2,2,128,64]{2,3,1,0:T(8,128)(2,1)}, bf16[2,2,128,64]{2,3,1,0:T(8,128)(2,1)}, u32[]{:S(2)}, u32[]{:S(2)}) collective-permute-start(bf16[2,2,128,64]{2,3,1,0:T(8,128)(2,1)} %pad_maximum_fusion.6), channel_id=1, source_target_pairs={{0,16},{1,17},{2,18},{3,19},{4,20},{5,21},{6,22},{7,23},{8,24},{9,... | collective-permute-start | bytes 196616 | tf_op jit(solution)/shard_map/ppermute | solution.py:151
  103.7 6.7 %all-to-all-start.1 = ((bf16[16,2,128,64]{2,3,1,0:T(8,128)(2,1)}), bf16[16,2,128,64]{2,3,1,0:T(8,128)(2,1)}, u32[]{:S(2)}, u32[]{:S(2)}) async-start(bf16[16,2,128,64]{2,3,1,0:T(8,128)(2,1)} %slice.218), calls=%async_computation.1 | async-start | bytes 1048576 | tf_op jit(solution)/shard_map/all_to_all | solution.py:78
  110.4 2.5 %reshape.489 = bf16[8,256,2,64]{3,2,1,0:T(2,128)(2,1)S(1)} reshape(bf16[2048,128]{1,0:T(8,128)(2,1)} %param.16) | data formatting | bytes 1048576 | tf_op jit(solution)/shard_map/vmap()/reshape;reshape | solution.py:17
  112.8 1.8 copy.126
  114.6 7.4 %reshape.485 = bf16[8,256,1024,1]{2,1,0,3:T(8,128)(2,1)} reshape(bf16[8,256,8,128]{3,2,1,0:T(8,128)(2,1)} %broadcast_multiply_fusion) | data formatting | bytes 8388608 | tf_op jit(solution)/shard_map/mul | solution.py:125
  123.5 6.5 %collective-permute-start.2 = (bf16[2,2,2,128,64]{3,4,2,0,1:T(8,128)(2,1)S(1)}, bf16[2,2,2,128,64]{3,4,2,0,1:T(8,128)(2,1)S(1)}, u32[]{:S(2)}, u32[]{:S(2)}) collective-permute-start(bf16[2,2,2,128,64]{3,4,2,0,1:T(8,128)(2,1)S(1)} %pad_maximum_fusion.5), channel_id=1, source_target_pairs={{0,8},{1,9},{2,10},{3,11},{4,12},{5,13},{6,14},{7,15},{8,0},{9,1},... | collective-permute-start | bytes 393224 | tf_op jit(solution)/shard_map/ppermute | solution.py:151
  130.7 12.0 %collective-permute-done.2 = bf16[2,2,2,128,64]{3,4,2,0,1:T(8,128)(2,1)S(1)} collective-permute-done((bf16[2,2,2,128,64]{3,4,2,0,1:T(8,128)(2,1)S(1)}, bf16[2,2,2,128,64]{3,4,2,0,1:T(8,128)(2,1)S(1)}, u32[]{:S(2)}, u32[]{:S(2)}) %collective-permute-start.2) | collective-permute-done | bytes 131104 | tf_op jit(solution)/shard_map/ppermute | solution.py:151
  142.8 2.1 %collective-permute-start.3 = (bf16[2,2,2,2,128,64]{4,5,3,0,1,2:T(8,128)(2,1)S(1)}, bf16[2,2,2,2,128,64]{4,5,3,0,1,2:T(8,128)(2,1)S(1)}, u32[]{:S(2)}, u32[]{:S(2)}) collective-permute-start(bf16[2,2,2,2,128,64]{4,5,3,0,1,2:T(8,128)(2,1)S(1)} %pad_maximum_fusion.4), channel_id=1, source_target_pairs={{0,4},{1,5},{2,6},{3,7},{4,0},{5,1},{6,2},{7,3},{8,12},{9,13},{10,... | collective-permute-start | bytes 786440 | tf_op jit(solution)/shard_map/ppermute | solution.py:151
  145.9 11.5 %collective-permute-done.3 = bf16[2,2,2,2,128,64]{4,5,3,0,1,2:T(8,128)(2,1)S(1)} collective-permute-done((bf16[2,2,2,2,128,64]{4,5,3,0,1,2:T(8,128)(2,1)S(1)}, bf16[2,2,2,2,128,64]{4,5,3,0,1,2:T(8,128)(2,1)S(1)}, u32[]{:S(2)}, u32[]{:S(2)}) %collective-permute-start.3) | collective-permute-done | bytes 262176 | tf_op jit(solution)/shard_map/ppermute | solution.py:151
  157.5 1.9 collective-permute-start.4
  159.5 1.8 fusion.44
  161.3 11.1 %collective-permute-done.4 = bf16[2,2,2,2,2,128,64]{5,6,4,0,1,2,3:T(8,128)(2,1)S(1)} collective-permute-done((bf16[2,2,2,2,2,128,64]{5,6,4,0,1,2,3:T(8,128)(2,1)S(1)}, bf16[2,2,2,2,2,128,64]{5,6,4,0,1,2,3:T(8,128)(2,1)S(1)}, u32[]{:S(2)}, u32[]{:S(2)}) %collective-permute-start.4) | collective-permute-done | bytes 524320 | tf_op jit(solution)/shard_map/ppermute | solution.py:151
  173.6 3.2 %collective-permute-start.5 = (bf16[2,2,2,2,2,2,128,64]{6,7,5,0,1,2,3,4:T(8,128)(2,1)}, bf16[2,2,2,2,2,2,128,64]{6,7,5,0,1,2,3,4:T(8,128)(2,1)}, u32[]{:S(2)}, u32[]{:S(2)}) collective-permute-start(bf16[2,2,2,2,2,2,128,64]{6,7,5,0,1,2,3,4:T(8,128)(2,1)} %pad_maximum_fusion.2), channel_id=1, source_target_pairs={{0,1},{1,0},{2,3},{3,2},{4,5},{5,4},{6,7},{7,6},{8,9},{9,8},{10,11... | collective-permute-start | bytes 3145736 | tf_op jit(solution)/shard_map/ppermute | solution.py:151
  177.0 1.5 fusion.53
  178.5 5.2 %fusion.13 = bf16[256,32,64]{0,2,1:T(8,128)(2,1)} fusion(f32[32,64,256]{2,1,0:T(8,128)S(1)} %fusion.53, bf16[256,32,64]{0,2,1:T(8,128)(2,1)} %bitcast.2, f32[256,256]{1,0:T(8,128)} %fusion.55, f32[32,256]{1,0:T(8,128)S(1)} %bitcast.254, f32[32,256]{1,0:T(8,128)S(1)} %copy_bitcast_fusion.1, pred[256,256]{1,0:T(8,128)(4,1)S(1)} %iota_compare_fusion.1, ...), kind=kOutput, calls=%fused_computation.22 | convolution fusion | flops 282066944 | bytes 4620416 | tf_op jit(solution)/shard_map/hij,jhp->ihp/dot_general | solution.py:10
  183.8 2.3 %copy.134 = bf16[1,256,2048]{2,1,0:T(8,128)(2,1)} copy(bf16[1,256,2048]{1,2,0:T(8,128)(2,1)} %bitcast.242) | data formatting | bytes 2097152
  186.0 1.4 select_bitcast_fusion.1
  187.7 2.2 %copy.129 = bf16[2,2,2,2,2,2,2,128,64]{7,5,4,3,2,1,0,8,6:T(2,128)(2,1)S(1)} copy(bf16[2,2,2,2,2,2,2,128,64]{7,8,6,0,1,2,3,4,5:T(8,128)(2,1)S(1)} %pad_maximum_fusion.1) | data formatting | bytes 4194304 | tf_op jit(solution)/shard_map/stack | solution.py:153
  192.3 1.5 fusion.26
  193.9 1.5 fusion.32
  (151 shorter events, 27.6 us)
Async XLA Ops:
  12.8 9.9 %copy-start.15 = (s32[384]{0:T(512)S(1)}, s32[384]{0:T(512)}, u32[]{:S(2)}) copy-start(s32[384]{0:T(512)} %param.22) | copy-start | bytes 4612
  12.8 9.8 %copy-start.16 = (s32[384]{0:T(512)S(1)}, s32[384]{0:T(512)}, u32[]{:S(2)}) copy-start(s32[384]{0:T(512)} %param.21) | copy-start | bytes 4612
  12.8 9.8 %copy-start.24 = (s32[1,8]{1,0:T(1,128)S(1)}, s32[1,8]{1,0:T(1,128)}, u32[]{:S(2)}) copy-start(s32[1,8]{1,0:T(1,128)} %param.20) | copy-start | bytes 100
  12.8 37.0 %copy-start.25 = (f32[32]{0:T(128)S(1)}, f32[32]{0:T(128)}, u32[]{:S(2)}) copy-start(f32[32]{0:T(128)} %param.23) | copy-start | bytes 388
  12.8 37.7 %copy-start.6 = (bf16[1,256,256]{2,1,0:T(8,128)(2,1)S(1)}, bf16[1,256,256]{2,1,0:T(8,128)(2,1)}, u32[]{:S(2)}) copy-start(bf16[1,256,256]{2,1,0:T(8,128)(2,1)} %param.13) | copy-start | bytes 393220
  14.4 39.7 %all-to-all-start = ((f32[16,2,136,64]{2,3,1,0:T(8,128)}), f32[16,2,136,64]{2,3,1,0:T(8,128)S(1)}, u32[]{:S(2)}, u32[]{:S(2)}) async-start(f32[16,2,136,64]{2,3,1,0:T(8,128)} %bitcast.5), calls=%async_computation | async-start | bytes 4194304 | tf_op jit(solution)/shard_map/all_to_all | solution.py:66
  22.0 34.9 %copy-start.1 = (bf16[2048,256]{1,0:T(8,128)(2,1)S(1)}, bf16[2048,256]{1,0:T(8,128)(2,1)}, u32[]{:S(2)}) copy-start(bf16[2048,256]{1,0:T(8,128)(2,1)} %param.17) | copy-start | bytes 3145732
  51.4 5.7 %copy-start.8 = (f32[2,2048]{1,0:T(2,128)S(1)}, f32[2,2048]{1,0:T(2,128)}, u32[]{:S(2)}) copy-start(f32[2,2048]{1,0:T(2,128)} %param.19) | copy-start | bytes 49156
  56.9 38.0 %copy-start.9 = (f32[2,2048]{1,0:T(2,128)S(1)}, f32[2,2048]{1,0:T(2,128)}, u32[]{:S(2)}) copy-start(f32[2,2048]{1,0:T(2,128)} %param.18) | copy-start | bytes 49156
  58.5 43.6 %copy-start.4 = (pred[8,256,256]{2,1,0:T(8,128)(4,1)S(1)}, pred[8,256,256]{2,1,0:T(8,128)(4,1)}, u32[]{:S(2)}) copy-start(pred[8,256,256]{2,1,0:T(8,128)(4,1)} %get-tuple-element.67) | copy-start | bytes 1572868
  58.7 36.9 %collective-permute-start = (bf16[2,128,64]{1,2,0:T(8,128)(2,1)S(1)}, bf16[2,128,64]{1,2,0:T(8,128)(2,1)S(1)}, u32[]{:S(2)}, u32[]{:S(2)}) collective-permute-start(bf16[2,128,64]{1,2,0:T(8,128)(2,1)S(1)} %slice_bitcast_fusion), channel_id=1, source_target_pairs={{0,32},{1,33},{2,34},{3,35},{4,36},{5,37},{6,38},{7,39},{8,40},{9,... | collective-permute-start | bytes 98312 | tf_op jit(solution)/shard_map/ppermute | solution.py:151
  95.6 19.1 %copy-start.10 = (f32[8,2,256]{2,0,1:T(8,128)S(1)}, f32[8,2,256]{2,0,1:T(8,128)}, u32[]{:S(2)}) copy-start(f32[8,2,256]{2,0,1:T(8,128)} %get-tuple-element.73) | copy-start | bytes 49156
  96.2 26.4 %collective-permute-start.1 = (bf16[2,2,128,64]{2,3,1,0:T(8,128)(2,1)}, bf16[2,2,128,64]{2,3,1,0:T(8,128)(2,1)}, u32[]{:S(2)}, u32[]{:S(2)}) collective-permute-start(bf16[2,2,128,64]{2,3,1,0:T(8,128)(2,1)} %pad_maximum_fusion.6), channel_id=1, source_target_pairs={{0,16},{1,17},{2,18},{3,19},{4,20},{5,21},{6,22},{7,23},{8,24},{9,... | collective-permute-start | bytes 196616 | tf_op jit(solution)/shard_map/ppermute | solution.py:151
  103.7 73.4 %all-to-all-start.1 = ((bf16[16,2,128,64]{2,3,1,0:T(8,128)(2,1)}), bf16[16,2,128,64]{2,3,1,0:T(8,128)(2,1)}, u32[]{:S(2)}, u32[]{:S(2)}) async-start(bf16[16,2,128,64]{2,3,1,0:T(8,128)(2,1)} %slice.218), calls=%async_computation.1 | async-start | bytes 1048576 | tf_op jit(solution)/shard_map/all_to_all | solution.py:78
  114.6 30.2 %copy-start.3 = (bf16[8,256,2,64]{1,3,2,0:T(8,128)(2,1)S(1)}, bf16[8,256,2,64]{1,3,2,0:T(8,128)(2,1)}, u32[]{:S(2)}) copy-start(bf16[8,256,2,64]{1,3,2,0:T(8,128)(2,1)} %copy.126) | copy-start | bytes 1572868
  123.5 19.2 %collective-permute-start.2 = (bf16[2,2,2,128,64]{3,4,2,0,1:T(8,128)(2,1)S(1)}, bf16[2,2,2,128,64]{3,4,2,0,1:T(8,128)(2,1)S(1)}, u32[]{:S(2)}, u32[]{:S(2)}) collective-permute-start(bf16[2,2,2,128,64]{3,4,2,0,1:T(8,128)(2,1)S(1)} %pad_maximum_fusion.5), channel_id=1, source_target_pairs={{0,8},{1,9},{2,10},{3,11},{4,12},{5,13},{6,14},{7,15},{8,0},{9,1},... | collective-permute-start | bytes 393224 | tf_op jit(solution)/shard_map/ppermute | solution.py:151
  142.8 14.6 %collective-permute-start.3 = (bf16[2,2,2,2,128,64]{4,5,3,0,1,2:T(8,128)(2,1)S(1)}, bf16[2,2,2,2,128,64]{4,5,3,0,1,2:T(8,128)(2,1)S(1)}, u32[]{:S(2)}, u32[]{:S(2)}) collective-permute-start(bf16[2,2,2,2,128,64]{4,5,3,0,1,2:T(8,128)(2,1)S(1)} %pad_maximum_fusion.4), channel_id=1, source_target_pairs={{0,4},{1,5},{2,6},{3,7},{4,0},{5,1},{6,2},{7,3},{8,12},{9,13},{10,... | collective-permute-start | bytes 786440 | tf_op jit(solution)/shard_map/ppermute | solution.py:151
  157.5 14.9 %collective-permute-start.4 = (bf16[2,2,2,2,2,128,64]{5,6,4,0,1,2,3:T(8,128)(2,1)S(1)}, bf16[2,2,2,2,2,128,64]{5,6,4,0,1,2,3:T(8,128)(2,1)S(1)}, u32[]{:S(2)}, u32[]{:S(2)}) collective-permute-start(bf16[2,2,2,2,2,128,64]{5,6,4,0,1,2,3:T(8,128)(2,1)S(1)} %pad_maximum_fusion.3), channel_id=1, source_target_pairs={{0,2},{1,3},{2,0},{3,1},{4,6},{5,7},{6,4},{7,5},{8,10},{9,11},{10,... | collective-permute-start | bytes 1572872 | tf_op jit(solution)/shard_map/ppermute | solution.py:151
  161.3 17.2 %copy-start.11 = (f32[1,32,256]{2,1,0:T(8,128)S(1)}, f32[1,32,256]{2,1,0:T(8,128)}, u32[]{:S(2)}) copy-start(f32[1,32,256]{2,1,0:T(8,128)} %param.14) | copy-start | bytes 98308
  161.3 17.3 %copy-start.12 = (f32[256,32]{0,1:T(8,128)S(1)}, f32[256,32]{0,1:T(8,128)}, u32[]{:S(2)}) copy-start(f32[256,32]{0,1:T(8,128)} %get-tuple-element.52) | copy-start | bytes 98308
  161.3 17.3 %copy-start.26 = (f32[32]{0:T(128)S(1)}, f32[32]{0:T(128)}, u32[]{:S(2)}) copy-start(f32[32]{0:T(128)} %param.23) | copy-start | bytes 388
  173.6 12.5 %collective-permute-start.5 = (bf16[2,2,2,2,2,2,128,64]{6,7,5,0,1,2,3,4:T(8,128)(2,1)}, bf16[2,2,2,2,2,2,128,64]{6,7,5,0,1,2,3,4:T(8,128)(2,1)}, u32[]{:S(2)}, u32[]{:S(2)}) collective-permute-start(bf16[2,2,2,2,2,2,128,64]{6,7,5,0,1,2,3,4:T(8,128)(2,1)} %pad_maximum_fusion.2), channel_id=1, source_target_pairs={{0,1},{1,0},{2,3},{3,2},{4,5},{5,4},{6,7},{7,6},{8,9},{9,8},{10,11... | collective-permute-start | bytes 3145736 | tf_op jit(solution)/shard_map/ppermute | solution.py:151
  187.4 2.5 %copy-start.18 = (pred[8]{0:T(512)(128)(4,1)S(1)}, pred[8]{0:T(512)(128)(4,1)}, u32[]{:S(2)}) copy-start(pred[8]{0:T(512)(128)(4,1)} %get-tuple-element.97) | copy-start | bytes 28
  187.4 2.5 %copy-start.19 = (pred[8]{0:T(512)(128)(4,1)S(1)}, pred[8]{0:T(512)(128)(4,1)}, u32[]{:S(2)}) copy-start(pred[8]{0:T(512)(128)(4,1)} %get-tuple-element.98) | copy-start | bytes 28
  187.4 2.5 %copy-start.20 = (pred[8]{0:T(512)(128)(4,1)S(1)}, pred[8]{0:T(512)(128)(4,1)}, u32[]{:S(2)}) copy-start(pred[8]{0:T(512)(128)(4,1)} %get-tuple-element.95) | copy-start | bytes 28
  187.4 2.5 %copy-start.21 = (pred[8]{0:T(512)(128)(4,1)S(1)}, pred[8]{0:T(512)(128)(4,1)}, u32[]{:S(2)}) copy-start(pred[8]{0:T(512)(128)(4,1)} %get-tuple-element.96) | copy-start | bytes 28
  187.4 2.5 %copy-start.22 = (pred[8]{0:T(512)(128)(4,1)S(1)}, pred[8]{0:T(512)(128)(4,1)}, u32[]{:S(2)}) copy-start(pred[8]{0:T(512)(128)(4,1)} %get-tuple-element.93) | copy-start | bytes 28
  187.5 2.5 %copy-start.23 = (pred[8]{0:T(512)(128)(4,1)S(1)}, pred[8]{0:T(512)(128)(4,1)}, u32[]{:S(2)}) copy-start(pred[8]{0:T(512)(128)(4,1)} %get-tuple-element.94) | copy-start | bytes 28
  187.5 2.5 %copy-start.27 = (s32[8]{0:T(128)S(1)}, s32[8]{0:T(128)}, u32[]{:S(2)}) copy-start(s32[8]{0:T(128)} %compare_select_fusion) | copy-start | bytes 100
  187.5 2.5 %copy-start.29 = (pred[8]{0:T(512)(128)(4,1)S(1)}, pred[8]{0:T(512)(128)(4,1)}, u32[]{:S(2)}) copy-start(pred[8]{0:T(512)(128)(4,1)} %iota_compare_fusion.13) | copy-start | bytes 28
  187.7 3.5 %copy-start.7 = (bf16[8,2,128,64]{2,3,1,0:T(8,128)(2,1)S(1)}, bf16[8,2,128,64]{2,3,1,0:T(8,128)(2,1)}, u32[]{:S(2)}) copy-start(bf16[8,2,128,64]{2,3,1,0:T(8,128)(2,1)} %constant_dynamic-update-slice_fusion) | copy-start | bytes 786436
  189.9 2.3 %copy-start = (bf16[8,256,1024,1]{2,1,0,3:T(8,128)(2,1)S(1)}, bf16[8,256,1024,1]{2,1,0,3:T(8,128)(2,1)}, u32[]{:S(2)}) copy-start(bf16[8,256,1024,1]{2,1,0,3:T(8,128)(2,1)} %reshape.485) | copy-start | bytes 12582916
  (6 other events, 9.8 us)
